TPU v7x, 512 devices: a whole 4x4x16 slice. The times are simulated.
512 devices in a mesh: dp: 32 (over x, z_lo, core), frame: 16 (over z_hi, y).
Axes of the slice: x: 4, y: 4, z: 16 (z_hi: 4, z_lo: 4; z = z_hi * 4 + z_lo), core: 2. Of those that a mesh axis runs over, the one named last changes fastest.
Arguments:
- queries: bfloat16 [32, 16, 128, 2048], P('dp', 'frame'), may hold values from -12 to 12
- key_states: bfloat16 [32, 16, 128, 2048], P('dp', 'frame'), may hold values from -6 to 6
- value_states: bfloat16 [32, 16, 128, 2048], P('dp', 'frame'), may hold values from -6 to 6
- head_scale: float32 [16], replicated, may hold values from 0.5 to 4
- out_weight: bfloat16 [2048, 3072], P('dp'), may hold values from -0.125 to 0.125
- frame_pattern: int32 [16, 2], replicated, may hold values from 0 to 15, as said below
- out_grad: bfloat16 [32, 16, 128, 3072], P('dp', 'frame'), may hold values from -6 to 6
Outputs:
- attended: bfloat16 [32, 16, 128, 3072], P('dp', 'frame')
- query_grad: bfloat16 [32, 16, 128, 2048], P('dp', 'frame')
- key_grad: bfloat16 [32, 16, 128, 2048], P('dp', 'frame')
- value_grad: bfloat16 [32, 16, 128, 2048], P('dp', 'frame')
- scale_grad: float32 [16], replicated
Inputs may be any that keep to these rules, and one draw needn't show every extreme that they name: `frame_pattern`: row f names 2 different frames, the first of them f itself.
All inputs are finite; a program needn't handle non-finite values.
Results may differ from a plain program's by a relative error of at most 0.0058.
Values may be sent and summed in bfloat16 or wider, within the bound.
A program may use at most 128 MiB of HBM per device.

v0:
```python
import math

import jax
import jax.numpy as jnp
from jax import lax
from jax.sharding import PartitionSpec as P

H = 16
HDH = 128


def local(queries, key_states, value_states, head_scale, out_weight, frame_pattern, out_grad):
    frame_count = lax.axis_size("frame")
    tokens = queries.shape[2]
    width = queries.shape[3]
    local_heads = width // HDH // frame_count
    slot_count = frame_pattern.shape[1]
    inv_root = 1.0 / math.sqrt(HDH)
    query_all, key_all, value_all = (
        lax.all_to_all(queries, "frame", split_axis=3, concat_axis=1, tiled=True),
        lax.all_to_all(key_states, "frame", split_axis=3, concat_axis=1, tiled=True),
        lax.all_to_all(value_states, "frame", split_axis=3, concat_axis=1, tiled=True),
    )
    query_heads = query_all.reshape(frame_count, tokens, local_heads, HDH)
    key_sel = key_all.reshape(frame_count, tokens, local_heads, HDH)[frame_pattern]
    key_sel = key_sel.reshape(frame_count, slot_count * tokens, local_heads, HDH)
    value_sel = value_all.reshape(frame_count, tokens, local_heads, HDH)[frame_pattern]
    value_sel = value_sel.reshape(frame_count, slot_count * tokens, local_heads, HDH)
    first_head = lax.axis_index("frame") * local_heads
    my_scale = lax.dynamic_slice_in_dim(head_scale, first_head, local_heads)
    factor = my_scale * inv_root
    plain_scores = jnp.einsum(
        "fthd,fkhd->fhtk", query_heads, key_sel, preferred_element_type=jnp.float32
    )
    probs = jax.nn.softmax(plain_scores * factor[None, :, None, None], axis=-1)
    probs_low = probs.astype(jnp.bfloat16)
    context = jnp.einsum(
        "fhtk,fkhd->fthd", probs_low, value_sel, preferred_element_type=jnp.float32
    ).astype(jnp.bfloat16)
    context = context.reshape(1, frame_count, tokens, local_heads * HDH)
    context_rows = lax.all_to_all(context, "frame", split_axis=1, concat_axis=3, tiled=True)
    full_weight = lax.all_gather(out_weight, "dp", axis=0, tiled=True)
    context_grad = lax.dot_general(
        out_grad[0, 0], full_weight, (((1,), (1,)), ((), ())), preferred_element_type=jnp.float32
    ).astype(jnp.bfloat16)
    grad_all = lax.all_to_all(
        context_grad[None, None], "frame", split_axis=3, concat_axis=1, tiled=True
    )
    attended = jnp.dot(context_rows[0, 0], full_weight, preferred_element_type=jnp.float32).astype(
        jnp.bfloat16
    )
    grad_heads = grad_all.reshape(frame_count, tokens, local_heads, HDH)
    prob_grad = jnp.einsum(
        "fthd,fkhd->fhtk", grad_heads, value_sel, preferred_element_type=jnp.float32
    )
    score_grad = probs * (prob_grad - jnp.sum(prob_grad * probs, axis=-1, keepdims=True))
    scale_part = jnp.sum(score_grad * plain_scores, axis=(0, 2, 3)) * inv_root
    score_low = score_grad.astype(jnp.bfloat16)
    query_grad = (
        jnp.einsum("fhtk,fkhd->fthd", score_low, key_sel, preferred_element_type=jnp.float32)
        * factor[None, None, :, None]
    )
    query_grad = query_grad.astype(jnp.bfloat16).reshape(1, frame_count, tokens, local_heads * HDH)
    key_part = (
        jnp.einsum("fhtk,fthd->fkhd", score_low, query_heads, preferred_element_type=jnp.float32)
        * factor[None, None, :, None]
    )
    key_part = key_part.reshape(frame_count, slot_count, tokens, local_heads * HDH)
    value_part = jnp.einsum(
        "fhtk,fthd->fkhd", probs_low, grad_heads, preferred_element_type=jnp.float32
    )
    value_part = value_part.reshape(frame_count, slot_count, tokens, local_heads * HDH)
    selector = (
        frame_pattern[None, :, :] == jnp.arange(frame_count, dtype=jnp.int32)[:, None, None]
    ).astype(jnp.float32)
    key_grad = jnp.einsum("gfs,fsud->gud", selector, key_part, precision=lax.Precision.HIGHEST)
    key_grad = key_grad.astype(jnp.bfloat16).reshape(1, frame_count, tokens, local_heads * HDH)
    value_grad = jnp.einsum("gfs,fsud->gud", selector, value_part, precision=lax.Precision.HIGHEST)
    value_grad = value_grad.astype(jnp.bfloat16).reshape(1, frame_count, tokens, local_heads * HDH)
    query_back, key_back, value_back = (
        lax.all_to_all(query_grad, "frame", split_axis=1, concat_axis=3, tiled=True),
        lax.all_to_all(key_grad, "frame", split_axis=1, concat_axis=3, tiled=True),
        lax.all_to_all(value_grad, "frame", split_axis=1, concat_axis=3, tiled=True),
    )
    offsets = jnp.arange(H, dtype=jnp.int32) - first_head
    picked = offsets[:, None] == jnp.arange(local_heads, dtype=jnp.int32)[None, :]
    scale_terms = jnp.sum(jnp.where(picked, scale_part[None, :], 0.0), axis=1)
    scale_grad = lax.psum(scale_terms, ("dp", "frame"))
    return (
        attended.reshape(1, 1, tokens, attended.shape[1]),
        query_back,
        key_back,
        value_back,
        scale_grad,
    )


def solution(mesh):
    return jax.shard_map(
        local,
        mesh=mesh,
        in_specs=(
            P("dp", "frame", None, None),
            P("dp", "frame", None, None),
            P("dp", "frame", None, None),
            P(),
            P("dp", None),
            P(),
            P("dp", "frame", None, None),
        ),
        out_specs=(
            P("dp", "frame", None, None),
            P("dp", "frame", None, None),
            P("dp", "frame", None, None),
            P("dp", "frame", None, None),
            P(),
        ),
        check_vma=False,
    )
```

profile of v0, /device:TPU:1, one launch (start us, length us, event | category | flops | bytes accessed | tf_op | source)
XLA Modules:
  0.0 482.5 jit_solution(17677016161023031074)
XLA Ops:
  7.9 2.4 copy.83
  10.8 11.5 %reduce.8 = bf16[2048,128]{1,0:T(8,128)(2,1)S(1)} reduce(bf16[2048,1,1,128]{3,2,1,0:T(2,128)(2,1)S(1)} %bitcast.157, bf16[]{:T(256)} %broadcast.58), dimensions={1,2}, to_apply=%bitcast.119.reduce_sub_computation | reduce | bytes 1048578
  23.2 18.4 %all-to-all-start = ((bf16[16,2,8192]{2,1,0:T(2,128)(2,1)}), bf16[16,2,8192]{2,1,0:T(2,128)(2,1)S(1)}, u32[]{:S(2)}, u32[]{:S(2)}) async-start(bf16[16,2,8192]{2,1,0:T(2,128)(2,1)} %reshape.178), calls=%async_computation | async-start | bytes 1048576 | tf_op jit(solution)/shard_map/all_to_all | solution.py:22
  42.4 11.6 %reduce.9 = bf16[2048,128]{1,0:T(8,128)(2,1)S(1)} reduce(bf16[2048,1,1,128]{3,2,1,0:T(2,128)(2,1)S(1)} %bitcast.159, bf16[]{:T(256)} %broadcast.58), dimensions={1,2}, to_apply=%bitcast.121.reduce_sub_computation | reduce | bytes 1048578
  54.9 21.3 %all-to-all-done = bf16[16,2,8192]{2,1,0:T(2,128)(2,1)S(1)} async-done(((bf16[16,2,8192]{2,1,0:T(2,128)(2,1)}), bf16[16,2,8192]{2,1,0:T(2,128)(2,1)S(1)}, u32[]{:S(2)}, u32[]{:S(2)}) %all-to-all-start) | async-done | bytes 524320 | tf_op jit(solution)/shard_map/all_to_all | solution.py:22
  76.3 18.7 %all-to-all-start.1 = ((bf16[16,2,8192]{2,1,0:T(2,128)(2,1)}), bf16[16,2,8192]{2,1,0:T(2,128)(2,1)S(1)}, u32[]{:S(2)}, u32[]{:S(2)}) async-start(bf16[16,2,8192]{2,1,0:T(2,128)(2,1)} %reshape.180), calls=%async_computation.1 | async-start | bytes 1048576 | tf_op jit(solution)/shard_map/all_to_all | solution.py:21
  95.8 11.5 %reduce.10 = bf16[2048,128]{1,0:T(8,128)(2,1)S(1)} reduce(bf16[2048,1,1,128]{3,2,1,0:T(2,128)(2,1)S(1)} %bitcast.160, bf16[]{:T(256)} %broadcast.58), dimensions={1,2}, to_apply=%bitcast.123.reduce_sub_computation | reduce | bytes 1048578
  108.2 21.2 %all-to-all-done.1 = bf16[16,2,8192]{2,1,0:T(2,128)(2,1)S(1)} async-done(((bf16[16,2,8192]{2,1,0:T(2,128)(2,1)}), bf16[16,2,8192]{2,1,0:T(2,128)(2,1)S(1)}, u32[]{:S(2)}, u32[]{:S(2)}) %all-to-all-start.1) | async-done | bytes 524320 | tf_op jit(solution)/shard_map/all_to_all | solution.py:21
  129.4 7.9 %all-to-all-start.2 = ((bf16[16,2,8192]{2,1,0:T(2,128)(2,1)}), bf16[16,2,8192]{2,1,0:T(2,128)(2,1)S(1)}, u32[]{:S(2)}, u32[]{:S(2)}) async-start(bf16[16,2,8192]{2,1,0:T(2,128)(2,1)} %reshape.182), calls=%async_computation.2 | async-start | bytes 1048576 | tf_op jit(solution)/shard_map/all_to_all | solution.py:20
  137.3 24.0 %all-gather.2.cloned.1.call-done = bf16[2048,3072]{1,0:T(8,128)(2,1)} async-done(((bf16[64,3072]{1,0:T(8,128)(2,1)}), bf16[2048,3072]{1,0:T(8,128)(2,1)}) %all-gather.2.cloned.1.call-update) | async-done | bytes 12582928 | tf_op jit(solution)/shard_map/all_gather | solution.py:42
  161.3 9.6 %fusion.2 = bf16[1,1,128,2048]{3,2,1,0:T(8,128)(2,1)} fusion(bf16[2048,3072]{1,0:T(8,128)(2,1)} %all-gather.2.cloned.1.call-done, bf16[1,1,128,3072]{3,2,1,0:T(8,128)(2,1)S(1)} %copy-done), kind=kOutput, calls=%fused_computation.6 | convolution fusion | flops 1610874880 | bytes 13893632 | tf_op jit(solution)/shard_map/dot_general | solution.py:43
  171.0 2.3 copy.93
  173.3 12.3 %reduce.11 = bf16[2048,128]{1,0:T(8,128)(2,1)} reduce(bf16[2048,1,1,128]{3,2,1,0:T(2,128)(2,1)S(1)} %bitcast.158, bf16[]{:T(256)} %broadcast.58), dimensions={1,2}, to_apply=%bitcast.125.reduce_sub_computation | reduce | bytes 1048578
  187.6 13.5 %all-to-all-start.4 = ((bf16[16,2,8192]{2,1,0:T(2,128)(2,1)}), bf16[16,2,8192]{2,1,0:T(2,128)(2,1)}, u32[]{:S(2)}, u32[]{:S(2)}) async-start(bf16[16,2,8192]{2,1,0:T(2,128)(2,1)} %reshape.184), calls=%async_computation.4 | async-start | bytes 1048576 | tf_op jit(solution)/shard_map/all_to_all | solution.py:46
  209.8 3.2 fusion.15
  213.1 7.5 %all-to-all-done.4 = bf16[16,2,8192]{2,1,0:T(2,128)(2,1)} async-done(((bf16[16,2,8192]{2,1,0:T(2,128)(2,1)}), bf16[16,2,8192]{2,1,0:T(2,128)(2,1)}, u32[]{:S(2)}, u32[]{:S(2)}) %all-to-all-start.4) | async-done | bytes 524320 | tf_op jit(solution)/shard_map/all_to_all | solution.py:46
  220.6 7.6 %all-to-all-start.3 = ((bf16[1,16,128,128]{2,3,0,1:T(8,128)(2,1)}), bf16[1,16,128,128]{2,3,0,1:T(8,128)(2,1)S(1)}, u32[]{:S(2)}, u32[]{:S(2)}) async-start(bf16[1,16,128,128]{2,3,0,1:T(8,128)(2,1)} %fusion.15), calls=%async_computation.3 | async-start | bytes 1048576 | tf_op jit(solution)/shard_map/all_to_all | solution.py:41
  228.2 2.2 reshape.185
  232.6 2.5 multiply_reduce_fusion
  238.0 6.4 %all-to-all-done.3 = bf16[1,16,128,128]{2,3,0,1:T(8,128)(2,1)S(1)} async-done(((bf16[1,16,128,128]{2,3,0,1:T(8,128)(2,1)}), bf16[1,16,128,128]{2,3,0,1:T(8,128)(2,1)S(1)}, u32[]{:S(2)}, u32[]{:S(2)}) %all-to-all-start.3) | async-done | bytes 524320 | tf_op jit(solution)/shard_map/all_to_all | solution.py:41
  244.4 7.5 %all-to-all-start.5 = ((bf16[1,16,128,128]{2,3,0,1:T(8,128)(2,1)}), bf16[1,16,128,128]{2,3,0,1:T(8,128)(2,1)S(1)}, u32[]{:S(2)}, u32[]{:S(2)}) async-start(bf16[1,16,128,128]{2,3,0,1:T(8,128)(2,1)} %fusion.20), calls=%async_computation.5 | async-start | bytes 1048576 | tf_op jit(solution)/shard_map/all_to_all | solution.py:81
  253.4 2.0 fusion.16
  256.3 16.6 %all-to-all-done.5 = bf16[1,16,128,128]{2,3,0,1:T(8,128)(2,1)S(1)} async-done(((bf16[1,16,128,128]{2,3,0,1:T(8,128)(2,1)}), bf16[1,16,128,128]{2,3,0,1:T(8,128)(2,1)S(1)}, u32[]{:S(2)}, u32[]{:S(2)}) %all-to-all-start.5) | async-done | bytes 524320 | tf_op jit(solution)/shard_map/all_to_all | solution.py:81
  273.0 6.7 %all-to-all-start.6 = ((bf16[1,16,128,128]{3,2,0,1:T(8,128)(2,1)}), bf16[1,16,128,128]{3,2,0,1:T(8,128)(2,1)}, u32[]{:S(2)}, u32[]{:S(2)}) async-start(bf16[1,16,128,128]{3,2,0,1:T(8,128)(2,1)} %copy.101), calls=%async_computation.6 | async-start | bytes 1048576 | tf_op jit(solution)/shard_map/all_to_all | solution.py:82
  279.7 3.4 convolution_bitcast_fusion
  283.0 2.3 reshape.143
  285.3 2.1 copy.105
  287.4 2.4 fusion.19
  290.8 14.8 %all-to-all-done.6 = bf16[1,16,128,128]{3,2,0,1:T(8,128)(2,1)} async-done(((bf16[1,16,128,128]{3,2,0,1:T(8,128)(2,1)}), bf16[1,16,128,128]{3,2,0,1:T(8,128)(2,1)}, u32[]{:S(2)}, u32[]{:S(2)}) %all-to-all-start.6) | async-done | bytes 524320 | tf_op jit(solution)/shard_map/all_to_all | solution.py:82
  305.6 7.6 %all-to-all-start.7 = ((bf16[1,16,128,128]{3,2,0,1:T(8,128)(2,1)}), bf16[1,16,128,128]{3,2,0,1:T(8,128)(2,1)S(1)}, u32[]{:S(2)}, u32[]{:S(2)}) async-start(bf16[1,16,128,128]{3,2,0,1:T(8,128)(2,1)} %copy.106), calls=%async_computation.7 | async-start | bytes 1048576 | tf_op jit(solution)/shard_map/all_to_all | solution.py:83
  313.9 7.3 %fusion.1 = bf16[1,1,128,3072]{3,2,1,0:T(8,128)(2,1)} fusion(bf16[128,2048]{0,1:T(8,128)(2,1)S(1)} %bitcast.161, bf16[2048,3072]{1,0:T(8,128)(2,1)} %all-gather.2.cloned.1.call-done), kind=kOutput, calls=%fused_computation.4 | convolution fusion | flops 1611005952 | bytes 13893632 | tf_op jit(solution)/shard_map/dot_general | solution.py:49
  321.3 149.4 %psum.7 = f32[16]{0:T(128)} all-reduce(f32[16]{0:T(128)S(1)} %compare_select_fusion.1), channel_id=1, replica_groups=mesh['dp'=32,'frame'=16] {'dp','frame'}, use_global_device_ids=true, to_apply=%region_4.5 | all-reduce | flops 16 | bytes 128 | tf_op jit(solution)/shard_map/psum | solution.py:88
  (63 shorter events, 28.4 us)
Async XLA Ops:
  7.2 154.2 %copy-start = (bf16[1,1,128,3072]{3,2,1,0:T(8,128)(2,1)S(1)}, bf16[1,1,128,3072]{3,2,1,0:T(8,128)(2,1)}, u32[]{:S(2)}) copy-start(bf16[1,1,128,3072]{3,2,1,0:T(8,128)(2,1)} %param.13) | copy-start | bytes 2359300
  7.2 154.2 %all-gather.2.cloned.1.call-start = ((), (), s32[]{:S(2)}) async-start(), calls=%async_computation.8 | async-start | bytes 12976128 | tf_op jit(solution)/shard_map/all_gather | solution.py:42
  10.3 31.4 %copy-start.6 = (bf16[1,1,128,2048]{3,2,1,0:T(8,128)(2,1)S(1)}, bf16[1,1,128,2048]{3,2,1,0:T(8,128)(2,1)}, u32[]{:S(2)}) copy-start(bf16[1,1,128,2048]{3,2,1,0:T(8,128)(2,1)} %param.8) | copy-start | bytes 1572868
  23.2 53.0 %all-to-all-start = ((bf16[16,2,8192]{2,1,0:T(2,128)(2,1)}), bf16[16,2,8192]{2,1,0:T(2,128)(2,1)S(1)}, u32[]{:S(2)}, u32[]{:S(2)}) async-start(bf16[16,2,8192]{2,1,0:T(2,128)(2,1)} %reshape.178), calls=%async_computation | async-start | bytes 1048576 | tf_op jit(solution)/shard_map/all_to_all | solution.py:22
  42.4 52.6 %copy-start.7 = (bf16[1,1,128,2048]{3,2,1,0:T(8,128)(2,1)S(1)}, bf16[1,1,128,2048]{3,2,1,0:T(8,128)(2,1)}, u32[]{:S(2)}) copy-start(bf16[1,1,128,2048]{3,2,1,0:T(8,128)(2,1)} %param.7) | copy-start | bytes 1572868
  76.3 53.2 %all-to-all-start.1 = ((bf16[16,2,8192]{2,1,0:T(2,128)(2,1)}), bf16[16,2,8192]{2,1,0:T(2,128)(2,1)S(1)}, u32[]{:S(2)}, u32[]{:S(2)}) async-start(bf16[16,2,8192]{2,1,0:T(2,128)(2,1)} %reshape.180), calls=%async_computation.1 | async-start | bytes 1048576 | tf_op jit(solution)/shard_map/all_to_all | solution.py:21
  129.4 58.2 %all-to-all-start.2 = ((bf16[16,2,8192]{2,1,0:T(2,128)(2,1)}), bf16[16,2,8192]{2,1,0:T(2,128)(2,1)S(1)}, u32[]{:S(2)}, u32[]{:S(2)}) async-start(bf16[16,2,8192]{2,1,0:T(2,128)(2,1)} %reshape.182), calls=%async_computation.2 | async-start | bytes 1048576 | tf_op jit(solution)/shard_map/all_to_all | solution.py:20
  173.3 27.9 %copy-start.8 = (s32[16,2]{0,1:T(2,128)S(1)}, s32[16,2]{0,1:T(2,128)}, u32[]{:S(2)}) copy-start(s32[16,2]{0,1:T(2,128)} %param.12) | copy-start | bytes 388
  173.3 28.1 %copy-start.9 = (f32[16]{0:T(128)S(1)}, f32[16]{0:T(128)}, u32[]{:S(2)}) copy-start(f32[16]{0:T(128)} %param.10) | copy-start | bytes 196
  187.6 32.9 %all-to-all-start.4 = ((bf16[16,2,8192]{2,1,0:T(2,128)(2,1)}), bf16[16,2,8192]{2,1,0:T(2,128)(2,1)}, u32[]{:S(2)}, u32[]{:S(2)}) async-start(bf16[16,2,8192]{2,1,0:T(2,128)(2,1)} %reshape.184), calls=%async_computation.4 | async-start | bytes 1048576 | tf_op jit(solution)/shard_map/all_to_all | solution.py:46
  207.8 5.3 %copy-start.4 = (bf16[1,1,128,16,128]{4,2,3,1,0:T(8,128)(2,1)}, bf16[1,1,128,16,128]{4,2,3,1,0:T(8,128)(2,1)S(1)}, u32[]{:S(2)}) copy-start(bf16[1,1,128,16,128]{4,2,3,1,0:T(8,128)(2,1)S(1)} %copy.89) | copy-start | bytes 1572868
  220.6 23.8 %all-to-all-start.3 = ((bf16[1,16,128,128]{2,3,0,1:T(8,128)(2,1)}), bf16[1,16,128,128]{2,3,0,1:T(8,128)(2,1)S(1)}, u32[]{:S(2)}, u32[]{:S(2)}) async-start(bf16[1,16,128,128]{2,3,0,1:T(8,128)(2,1)} %fusion.15), calls=%async_computation.3 | async-start | bytes 1048576 | tf_op jit(solution)/shard_map/all_to_all | solution.py:41
  232.6 2.5 copy-start.5
  232.6 2.7 copy-start.10
  244.4 28.6 %all-to-all-start.5 = ((bf16[1,16,128,128]{2,3,0,1:T(8,128)(2,1)}), bf16[1,16,128,128]{2,3,0,1:T(8,128)(2,1)S(1)}, u32[]{:S(2)}, u32[]{:S(2)}) async-start(bf16[1,16,128,128]{2,3,0,1:T(8,128)(2,1)} %fusion.20), calls=%async_computation.5 | async-start | bytes 1048576 | tf_op jit(solution)/shard_map/all_to_all | solution.py:81
  253.4 26.3 %copy-start.1 = (bf16[1,1,128,2048]{2,3,0,1:T(8,128)(2,1)S(1)}, bf16[1,1,128,2048]{2,3,0,1:T(8,128)(2,1)}, u32[]{:S(2)}) copy-start(bf16[1,1,128,2048]{2,3,0,1:T(8,128)(2,1)} %copy.125) | copy-start | bytes 1572868
  273.0 6.7 %copy-start.2 = (bf16[1,16,128,128]{2,3,0,1:T(8,128)(2,1)}, bf16[1,16,128,128]{2,3,0,1:T(8,128)(2,1)S(1)}, u32[]{:S(2)}) copy-start(bf16[1,16,128,128]{2,3,0,1:T(8,128)(2,1)S(1)} %all-to-all-done.5) | copy-start | bytes 1572868
  273.0 32.6 %all-to-all-start.6 = ((bf16[1,16,128,128]{3,2,0,1:T(8,128)(2,1)}), bf16[1,16,128,128]{3,2,0,1:T(8,128)(2,1)}, u32[]{:S(2)}, u32[]{:S(2)}) async-start(bf16[1,16,128,128]{3,2,0,1:T(8,128)(2,1)} %copy.101), calls=%async_computation.6 | async-start | bytes 1048576 | tf_op jit(solution)/shard_map/all_to_all | solution.py:82
  305.6 168.4 %all-to-all-start.7 = ((bf16[1,16,128,128]{3,2,0,1:T(8,128)(2,1)}), bf16[1,16,128,128]{3,2,0,1:T(8,128)(2,1)S(1)}, u32[]{:S(2)}, u32[]{:S(2)}) async-start(bf16[1,16,128,128]{3,2,0,1:T(8,128)(2,1)} %copy.106), calls=%async_computation.7 | async-start | bytes 1048576 | tf_op jit(solution)/shard_map/all_to_all | solution.py:83
  313.9 156.7 %copy-start.3 = (bf16[1,16,128,128]{2,3,0,1:T(8,128)(2,1)S(1)}, bf16[1,16,128,128]{2,3,0,1:T(8,128)(2,1)}, u32[]{:S(2)}) copy-start(bf16[1,16,128,128]{2,3,0,1:T(8,128)(2,1)} %copy-done.2) | copy-start | bytes 1572868
Sparse Core Ops, SparseCore 0:
  10.2 151.1 all-gather.1
where the time goes:
time: 492 us; the launch traced here: 482 us
  blocking collectives  149 us (30%)
  waiting for transfers between devices  113 us (23%)
  starting transfers between devices  87.9 us (18%)
  other arithmetic  47 us (10%)
  matrix products  36.7 us (7%)
  local copies, waits for them, and re-layouts  32.8 us (7%)
  between operations  16.2 us (3%)
    psum x1, blocking collectives, local(): scale_grad = lax.psum(scale_terms, ('dp', 'frame'))  149 us
    unnamed x4, other arithmetic  47 us
    all_gather x1, waiting for transfers between devices, local(): full_weight = lax.all_gather(out_weight, 'dp', axis=0, tiled=True)  24 us
    all_to_all x1, waiting for transfers between devices, local(): lax.all_to_all(value_states, 'frame', split_axis=3, concat_axis=1, tiled=...  21.3 us
    all_to_all x1, waiting for transfers between devices, local(): lax.all_to_all(key_states, 'frame', split_axis=3, concat_axis=1, tiled=True)  21.2 us
    all_to_all x1, starting transfers between devices, local(): lax.all_to_all(key_states, 'frame', split_axis=3, concat_axis=1, tiled=True)  18.7 us
    all_to_all x1, starting transfers between devices, local(): lax.all_to_all(value_states, 'frame', split_axis=3, concat_axis=1, tiled=...  18.4 us
    unnamed x41, local copies, waits for them, and re-layouts  17.3 us
  transfers between devices with their start and end apart: 9, of which 7 were waited for; matrix products, arithmetic and copies ran while one was open for 24% of the time, Pallas kernels for 0%

commit v1 on v0

v1 whole, which is shorter than its diff:
```python
import math

import jax
import jax.numpy as jnp
from jax import lax
from jax.experimental import pallas as pl
from jax.experimental.pallas import tpu as pltpu
from jax.sharding import PartitionSpec as P

MESH = pl.DeviceIdType.MESH
F = 16
T = 128
HDH = 128
D = 3072
HALF = D // 2
BF16 = jnp.bfloat16
F32 = jnp.float32

A, B1Y, B1X, Q, K, V, CG, CX, QG, KG, VG = range(11)
B2X, B2Y, SIB, RED = 11, 14, 17, 25
N_SEM = 30
NT = (((1,), (1,)), ((), ()))
TN = (((0,), (0,)), ((), ()))


def body(
    pat, scale, q, k, v, og, w, att, qg, kg, vg, sg,
    wv, ogv, qb, kb, vb, cb, cgo, cxo, cxr, qo, ko, vo, kp, vp, plain, probs, attv, red, redo,
    ss, rs, ls,
):
    d, f = lax.axis_index("dp"), lax.axis_index("frame")
    x, zl, core = d // 8, lax.rem(d // 2, 4), lax.rem(d, 2)
    zh, y = f // 4, lax.rem(f, 4)
    z = zh * 4 + zl

    def at_frame(i):
        return (d, lax.rem(f + i, F))

    def at_x(i):
        return (lax.rem(x + i + 4, 4) * 8 + lax.rem(d, 8), f)

    def at_y(i):
        return (d, zh * 4 + lax.rem(y + i + 4, 4))

    def at_zh(i):
        return (d, lax.rem(zh + i + 4, 4) * 4 + y)

    def at_z(i):
        there = lax.rem(z + i + 16, 16)
        return (x * 8 + lax.rem(there, 4) * 2 + core, (there // 4) * 4 + y)

    sibling = (d + 1 - 2 * core, f)

    def send(src, dst, sem, device, recv=None):
        pltpu.make_async_remote_copy(
            src, dst, ss.at[sem], rs.at[sem if recv is None else recv], device_id=device, device_id_type=MESH
        ).start()

    def arrive(sem, ref):
        pltpu.make_async_copy(ref, ref, rs.at[sem]).wait()

    def sent(sem, ref):
        pltpu.make_async_copy(ref, ref, ss.at[sem]).wait()

    barrier = pltpu.get_barrier_semaphore()
    peers = [at_x(i) for i in (1, 2, 3)] + [at_z(i) for i in (1, -1, 2, -2)] + [sibling]

    @pl.loop(1, F)
    def _(i):
        pl.semaphore_signal(barrier, inc=1, device_id=at_frame(i), device_id_type=MESH)

    for peer in peers:
        pl.semaphore_signal(barrier, inc=1, device_id=peer, device_id_type=MESH)
    pl.semaphore_wait(barrier, F - 1 + len(peers))

    rows = pl.ds(pl.multiple_of(y * 16, 16), 16)
    first, second = pl.ds(0, HALF), pl.ds(HALF, HALF)
    mine = pl.ds(pl.multiple_of(f * HDH, HDH), HDH)

    for i in (1, -1, 2):
        send(w.at[rows], wv.at[x, zl, core, rows], A, at_z(i))
    pltpu.make_async_copy(w.at[rows], wv.at[x, zl, core, rows], rs.at[A]).start()
    pltpu.make_async_copy(og, ogv, ls.at[0]).start()

    def scatter(src, dst, sem):
        @pl.loop(1, F)
        def _(i):
            there = lax.rem(f + i, F)
            send(src.at[:, pl.ds(pl.multiple_of(there * HDH, HDH), HDH)], dst.at[f], sem, (d, there))

        pltpu.make_async_copy(src.at[:, mine], dst.at[f], rs.at[sem]).start()

    scatter(q, qb, Q)

    arrive(A, wv.at[x, :, core, rows])
    for i in (1, 2, 3):
        send(wv.at[x, :, core, rows, first], wv.at[x, :, core, rows, first], B1Y, at_y(i))
        send(wv.at[x, :, core, rows, second], wv.at[x, :, core, rows, second], B1X, at_x(i))
    scatter(k, kb, K)

    arrive(B1Y, wv.at[x, :, core, pl.ds(0, 48), first])
    for i in (1, 2, 3):
        send(wv.at[x, :, core, :, first], wv.at[x, :, core, :, first], B2X + i - 1, at_x(i))
    send(wv.at[x, :, core, :, first], wv.at[x, :, core, :, first], SIB, sibling)
    arrive(B1X, wv.at[pl.ds(0, 3), :, core, rows, second])
    for i in (1, 2, 3):
        send(wv.at[:, :, core, rows, second], wv.at[:, :, core, rows, second], B2Y + i - 1, at_y(i))
    send(wv.at[:, :, core, rows, second], wv.at[:, :, core, rows, second], SIB + 1, sibling)
    scatter(v, vb, V)

    for i in (1, 2, 3):
        there = lax.rem(x - i + 4, 4)
        piece = wv.at[there, :, core, :, first]
        arrive(B2X + i - 1, piece)
        send(piece, piece, SIB + 1 + i, sibling)
        there = pl.ds(pl.multiple_of(lax.rem(y - i + 4, 4) * 16, 16), 16)
        piece = wv.at[:, :, core, there, second]
        arrive(B2Y + i - 1, piece)
        send(piece, piece, SIB + 4 + i, sibling)
    for i in range(8):
        arrive(SIB + i, wv.at[0, :, core, :, first])
    pltpu.make_async_copy(og, ogv, ls.at[0]).wait()

    def context_grad(pair):
        two = wv[pair // 2, pl.ds(lax.rem(pair, 2) * 2, 2)].reshape(2 * HDH, D)
        made = lax.dot_general(ogv[...], two, NT, preferred_element_type=F32).astype(BF16)
        return made[:, :HDH], made[:, HDH:]

    @pl.loop(1, F // 2)
    def _(i):
        pair = lax.rem(f // 2 + i, F // 2)
        even, odd = context_grad(pair)
        cgo[2 * pair] = even
        send(cgo.at[2 * pair], cb.at[f], CG, (d, 2 * pair))
        cgo[2 * pair + 1] = odd
        send(cgo.at[2 * pair + 1], cb.at[f], CG, (d, 2 * pair + 1))

    own, other = f, f + 1 - 2 * lax.rem(f, 2)
    even, odd = context_grad(f // 2)
    cgo[2 * (f // 2)] = even
    cgo[2 * (f // 2) + 1] = odd
    send(cgo.at[other], cb.at[f], CG, (d, other))
    cb[f] = cgo[own]

    inv_root = 1.0 / math.sqrt(HDH)
    factor = scale[f] * inv_root
    for sem, ref in ((Q, qb), (K, kb), (V, vb)):
        arrive(sem, ref)

    def both(ref, t):
        return jnp.concatenate([ref[t], ref[pat[t, 1]]], axis=0)

    def forward(t):
        scores = lax.dot_general(both(kb, t), qb[t], NT, preferred_element_type=F32)
        plain[t] = scores
        scaled = scores * factor
        e = jnp.exp(scaled - jnp.max(scaled, axis=0, keepdims=True))
        p = e / jnp.sum(e, axis=0, keepdims=True)
        probs[t] = p
        return lax.dot_general(p.astype(BF16), both(vb, t), TN, preferred_element_type=F32).astype(BF16)

    @pl.loop(1, F)
    def _(i):
        t = lax.rem(f + i, F)
        cxo[t] = forward(t)
        send(cxo.at[t], cxr.at[:, mine], CX, (d, t))

    cxr[:, mine] = forward(f)

    arrive(CG, cb.at[pl.ds(0, F - 1)])

    def backward(t):
        p = probs[t]
        gain = cb[t]
        prob_grad = lax.dot_general(both(vb, t), gain, NT, preferred_element_type=F32)
        score_grad = p * (prob_grad - jnp.sum(prob_grad * p, axis=0, keepdims=True))
        term = jnp.sum((score_grad * plain[t]).reshape(32, 8, HDH), axis=0)
        low = score_grad.astype(BF16)
        query = lax.dot_general(low, both(kb, t), TN, preferred_element_type=F32) * factor
        key = jnp.dot(low, qb[t], preferred_element_type=F32) * factor
        value = jnp.dot(p.astype(BF16), gain, preferred_element_type=F32)
        kp[0, t], kp[1, t] = key[:T], key[T:]
        vp[0, t], vp[1, t] = value[:T], value[T:]
        qo[t] = query.astype(BF16)
        return term

    redo[0] = jnp.zeros((8, HDH), F32)

    @pl.loop(1, F)
    def _(i):
        t = lax.rem(f + i, F)
        redo[0] += backward(t)
        send(qo.at[t], qg.at[:, mine], QG, (d, t))

    total = jnp.sum(redo[0] + backward(f), keepdims=True) * inv_root
    pltpu.make_async_copy(qo.at[f], qg.at[:, mine], ls.at[1]).start()

    lanes = lax.broadcasted_iota(jnp.int32, (8, HDH), 1)
    stages = (
        (2, core, [sibling]),
        (4, x, [at_x(i) for i in (1, 2, 3)]),
        (4, y, [at_y(i) for i in (1, 2, 3)]),
        (4, zh, [at_zh(i) for i in (1, 2, 3)]),
        (4, zl, [at_z(i) for i in (1, -1, 2)]),
    )

    def give(s, value):
        _, here, devices = stages[s]
        redo[s + 1] = value
        red[s, here] = value
        for device in devices:
            send(redo.at[s + 1], red.at[s, here], RED + s, device)

    def take(s):
        n, _, devices = stages[s]
        arrive(RED + s, red.at[s, pl.ds(0, len(devices))])
        return sum(red[s, j] for j in range(1, n)) + red[s, 0]

    give(0, jnp.where(lanes == f, total, 0.0))

    def gather(part, out, dst, sem, local):
        def one(g):
            acc = part[0, g]
            for t in range(F):
                acc += jnp.where(pat[t, 1] == g, 1.0, 0.0) * part[1, t]
            out[g] = acc.astype(BF16)

        @pl.loop(1, F)
        def _(i):
            g = lax.rem(f + i, F)
            one(g)
            send(out.at[g], dst.at[:, mine], sem, (d, g))

        one(f)
        pltpu.make_async_copy(out.at[f], dst.at[:, mine], ls.at[local]).start()

    gather(kp, ko, kg, KG, 2)
    give(1, take(0))
    gather(vp, vo, vg, VG, 3)
    give(2, take(1))

    arrive(CX, cxr.at[:, pl.ds(0, (F - 1) * HDH)])
    width = 512

    @pl.loop(0, D // width)
    def _(n):
        cols = pl.ds(pl.multiple_of(n * width, width), width)
        block = wv[:, :, :, :, cols].reshape(F * HDH, width)
        attv[:, cols] = jnp.dot(cxr[...], block, preferred_element_type=F32).astype(BF16)

    pltpu.make_async_copy(attv, att, ls.at[4]).start()
    give(3, take(2))
    give(4, take(3))
    sg[...] = take(4)[:1, :F]

    for sem, ref in ((QG, qg), (KG, kg), (VG, vg)):
        arrive(sem, ref.at[:, pl.ds(0, (F - 1) * HDH)])
    for j, (src, dst) in enumerate(((qo, qg), (ko, kg), (vo, vg))):
        pltpu.make_async_copy(src.at[f], dst.at[:, mine], ls.at[j + 1]).wait()
    pltpu.make_async_copy(attv, att, ls.at[4]).wait()
    for sem, ref in ((Q, qb), (K, kb), (V, vb), (CG, cgo), (CX, cxo), (QG, qo), (KG, ko), (VG, vo)):
        sent(sem, ref.at[pl.ds(0, F - 1)])
    sent(A, wv.at[0, pl.ds(0, 3), 0, pl.ds(0, 16)])
    sent(B1Y, wv.at[0, :, 0, pl.ds(0, 48), first])
    sent(B1X, wv.at[pl.ds(0, 3), :, 0, pl.ds(0, 16), second])
    for i in range(3):
        sent(B2X + i, wv.at[0, :, 0, :, first])
        sent(B2Y + i, wv.at[:, :, 0, pl.ds(0, 16), second])
    for i in range(8):
        sent(SIB + i, wv.at[0, :, 0, :, first])
    for s, (_, _, devices) in enumerate(stages):
        sent(RED + s, red.at[s, pl.ds(0, len(devices))])


def local(queries, key_states, value_states, head_scale, out_weight, frame_pattern, out_grad):
    anywhere = pl.BlockSpec(memory_space=pl.ANY)
    scalars = pl.BlockSpec(memory_space=pltpu.SMEM)
    slots = pltpu.VMEM((F, T, HDH), BF16)
    parts = pltpu.VMEM((2, F, T, HDH), F32)
    square = pltpu.VMEM((F, 2 * T, T), F32)
    row = jax.ShapeDtypeStruct((T, F * HDH), BF16)
    attended, query_grad, key_grad, value_grad, scale_grad = pl.pallas_call(
        body,
        out_shape=(
            jax.ShapeDtypeStruct((T, D), BF16),
            row,
            row,
            row,
            jax.ShapeDtypeStruct((1, F), F32),
        ),
        in_specs=[scalars, scalars] + [anywhere] * 5,
        out_specs=[anywhere] * 4 + [pl.BlockSpec(memory_space=pltpu.VMEM)],
        scratch_shapes=[
            pltpu.VMEM((4, 4, 2, 64, D), BF16),
            pltpu.VMEM((T, D), BF16),
            slots, slots, slots, slots,
            slots, slots,
            pltpu.VMEM((T, F * HDH), BF16),
            slots, slots, slots,
            parts, parts,
            square, square,
            pltpu.VMEM((T, D), BF16),
            pltpu.VMEM((5, 4, 8, HDH), F32),
            pltpu.VMEM((6, 8, HDH), F32),
            pltpu.SemaphoreType.DMA((N_SEM,)),
            pltpu.SemaphoreType.DMA((N_SEM,)),
            pltpu.SemaphoreType.DMA((5,)),
        ],
        compiler_params=pltpu.CompilerParams(
            collective_id=0, has_side_effects=True, vmem_limit_bytes=56 << 20
        ),
    )(
        frame_pattern,
        head_scale,
        queries[0, 0],
        key_states[0, 0],
        value_states[0, 0],
        out_grad[0, 0],
        out_weight,
    )
    return (
        attended[None, None],
        query_grad[None, None],
        key_grad[None, None],
        value_grad[None, None],
        scale_grad.reshape(F),
    )


def solution(mesh):
    rows = P("dp", "frame", None, None)
    return jax.shard_map(
        local,
        mesh=mesh,
        in_specs=(rows, rows, rows, P(), P("dp", None), P(), rows),
        out_specs=(rows, rows, rows, rows, P()),
        check_vma=False,
    )
```

time: 492 us -> 242 us (0.49)
  the two profiles are of different devices: /device:TPU:1 before, /device:TPU:22 now
where the time goes in v1:
time: 242 us
  Pallas kernels  234 us (97%)
  local copies, waits for them, and re-layouts  7.24 us (3%)
    pallas_call x1, Pallas kernels, local(): pl.pallas_call(body, out_shape=(jax.ShapeDtypeStruct((T, D), BF16), row,...  234 us
    unnamed x16, local copies, waits for them, and re-layouts  7.24 us

profile of v1, /device:TPU:22, one launch (start us, length us, event | category | flops | bytes accessed | tf_op | source)
XLA Modules:
  0.0 241.8 jit_solution(14441219492356503014)
XLA Ops:
  0.6 0.0 copy-start.3
  0.6 0.7 copy-done.3
  1.3 0.7 copy.12.pat
  2.0 233.9 %shard_map.110 = (bf16[128,3072]{1,0:T(8,128)(2,1)}, bf16[128,2048]{1,0:T(8,128)(2,1)}, bf16[128,2048]{1,0:T(8,128)(2,1)}, bf16[128,2048]{1,0:T(8,128)(2,1)}, f32[1,16]{1,0:T(1,128)}) custom-call(s32[16,2]{1,0:T(8,128)} %copy.12.pat, f32[16]{0:T(128)} %scale.1, bf16[128,2048]{1,0:T(8,128)(2,1)} %bitcast.14, bf16[128,2048]{1,0:T(8,128)(2,1)} %bitcast.15, ...), custom_call_target="tpu_custom_call" | custom-call | tf_op jit(solution)/shard_map/pallas_call | solution.py:282
  235.9 0.0 copy-start.2
  235.9 2.1 copy.18
  238.1 0.0 copy-done.2
  238.1 0.0 copy-start.1
  238.1 0.8 copy.19
  238.9 0.4 copy-done.1
  239.3 0.0 copy-start
  239.3 0.8 copy.20
  240.1 0.4 copy-done
  240.5 0.0 copy-start.4
  240.5 0.8 copy.21
  241.3 0.0 copy-done.4
  241.3 0.5 copy.22
Async XLA Ops:
  0.6 0.7 copy-start.3
  235.9 2.1 copy-start.2
  238.1 1.2 copy-start.1
  239.3 1.2 copy-start
  240.5 0.8 copy-start.4

commit v2 on v1

v2 whole, which is shorter than its diff:
```python
import math

import jax
import jax.numpy as jnp
from jax import lax
from jax.experimental import pallas as pl
from jax.experimental.pallas import tpu as pltpu
from jax.sharding import PartitionSpec as P

MESH = pl.DeviceIdType.MESH
F = 16
T = 128
HDH = 128
D = 3072
HALF = D // 2
BF16 = jnp.bfloat16
F32 = jnp.float32

A, B1Y, B1X, OG, Q, K, V, CG, CX, ATT, QG, KG, VG = range(13)
B2X, B2Y, RED = 13, 16, 19
N_SEM = 24
NT = (((1,), (1,)), ((), ()))
TN = (((0,), (0,)), ((), ()))


def body(
    pat, scale, q, k, v, og, w, att, qg, kg, vg, sg,
    wv, ogv, qb, kb, vb, cb, cgo, cxo, cxr, qo, ko, vo, kp, vp, plain, probs, attp, attr, attv, red, redo,
    ss, rs, ls,
):
    d, f = lax.axis_index("dp"), lax.axis_index("frame")
    x, zl, core = d // 8, lax.rem(d // 2, 4), lax.rem(d, 2)
    zh, y = f // 4, lax.rem(f, 4)
    z = zh * 4 + zl

    def at_frame(i):
        return (d, lax.rem(f + i, F))

    def at_x(i):
        return (lax.rem(x + i + 4, 4) * 8 + lax.rem(d, 8), f)

    def at_y(i):
        return (d, zh * 4 + lax.rem(y + i + 4, 4))

    def at_zh(i):
        return (d, lax.rem(zh + i + 4, 4) * 4 + y)

    def at_z(i, c=core):
        there = lax.rem(z + i + 16, 16)
        return (x * 8 + lax.rem(there, 4) * 2 + c, (there // 4) * 4 + y)

    sibling = (d + 1 - 2 * core, f)

    def on_core(c, t):
        return (d - core + c, t)

    def turn(i):
        m = lax.rem(i, 4)
        dz = 1 + 2 * m - 3 * (m // 2)
        return lax.rem(zh + dz, 4) * 4 + lax.rem(y + 1 + i // 4, 4)

    def send(src, dst, sem, device, recv=None):
        pltpu.make_async_remote_copy(
            src, dst, ss.at[sem], rs.at[sem if recv is None else recv], device_id=device, device_id_type=MESH
        ).start()

    def arrive(sem, ref):
        pltpu.make_async_copy(ref, ref, rs.at[sem]).wait()

    def sent(sem, ref):
        pltpu.make_async_copy(ref, ref, ss.at[sem]).wait()

    barrier = pltpu.get_barrier_semaphore()
    peers = [at_x(i) for i in (1, 2, 3)] + [at_z(i, c) for i in (1, -1, 2, -2) for c in (0, 1)] + [sibling]

    @pl.loop(1, F)
    def _(i):
        t = lax.rem(f + i, F)
        for c in (0, 1):
            pl.semaphore_signal(barrier, inc=1, device_id=on_core(c, t), device_id_type=MESH)

    for peer in peers:
        pl.semaphore_signal(barrier, inc=1, device_id=peer, device_id_type=MESH)
    pl.semaphore_wait(barrier, 2 * (F - 1) + len(peers))

    rows = pl.ds(pl.multiple_of(y * 16, 16), 16)
    first, second = pl.ds(0, HALF), pl.ds(HALF, HALF)
    mine = pl.ds(pl.multiple_of(f * HDH, HDH), HDH)

    keeper = zl // 2
    quarter = wv.at[x, lax.rem(zl, 2), core, rows]
    for i in (1, -1, 2):
        send(w.at[rows], quarter, A, at_z(i, keeper))

    @pl.when(core == keeper)
    def _():
        pltpu.make_async_copy(w.at[rows], quarter, rs.at[A]).start()

    @pl.when(core != keeper)
    def _():
        send(w.at[rows], quarter, A, sibling)

    pltpu.make_async_copy(og, ogv.at[core], ls.at[0]).start()
    send(og, ogv.at[core], OG, sibling)

    def scatter(src, dst, sem):
        @pl.loop(0, F - 1)
        def _(i):
            there = turn(i)
            send(src.at[:, pl.ds(pl.multiple_of(there * HDH, HDH), HDH)], dst.at[f], sem, (d, there))

        pltpu.make_async_copy(src.at[:, mine], dst.at[f], rs.at[sem]).start()

    scatter(q, qb, Q)

    arrive(A, wv.at[x, :, :, rows])
    for i in (1, 2, 3):
        send(wv.at[x, :, :, rows, first], wv.at[x, :, :, rows, first], B1Y, at_y(i))
        send(wv.at[x, :, :, rows, second], wv.at[x, :, :, rows, second], B1X, at_x(i))
    scatter(k, kb, K)

    arrive(B1Y, wv.at[x, :, :, pl.ds(0, 48), first])
    for i in (1, 2, 3):
        send(wv.at[x, :, :, :, first], wv.at[x, :, :, :, first], B2X + i - 1, at_x(i))
    arrive(B1X, wv.at[pl.ds(0, 3), :, :, rows, second])
    for i in (1, 2, 3):
        send(wv.at[:, :, :, rows, second], wv.at[:, :, :, rows, second], B2Y + i - 1, at_y(i))
    scatter(v, vb, V)

    inv_root = 1.0 / math.sqrt(HDH)
    factor = scale[f] * inv_root

    here = pl.ds(pl.multiple_of((zh * 2 + lax.rem(y, 2)) * HDH, HDH), HDH)

    def both(ref, t):
        return jnp.concatenate([ref[t], ref[pat[1, t]]], axis=0)

    arrive(Q, qb)
    arrive(K, kb)

    @pl.loop(0, F)
    def _(t):
        scores = lax.dot_general(both(kb, t), qb[t], NT, preferred_element_type=F32)
        plain[t] = scores
        scaled = scores * factor
        e = jnp.exp(scaled - jnp.max(scaled, axis=0, keepdims=True))
        probs[t] = e / jnp.sum(e, axis=0, keepdims=True)

    arrive(V, vb)

    def forward(t):
        return lax.dot_general(probs[t].astype(BF16), both(vb, t), TN, preferred_element_type=F32).astype(BF16)

    @pl.loop(0, F - 1)
    def _(i):
        t = turn(i)
        cxo[t] = forward(t)
        send(cxo.at[t], cxr.at[core, :, here], CX, on_core(y // 2, t))

    cxo[f] = forward(f)

    @pl.when(core == y // 2)
    def _():
        pltpu.make_async_copy(cxo.at[f], cxr.at[core, :, here], rs.at[CX]).start()

    @pl.when(core != y // 2)
    def _():
        send(cxo.at[f], cxr.at[core, :, here], CX, sibling)

    for i in (1, 2, 3):
        arrive(B2X + i - 1, wv.at[0, :, :, :, first])
        arrive(B2Y + i - 1, wv.at[:, :, :, pl.ds(0, 16), second])
    pltpu.make_async_copy(og, ogv.at[core], ls.at[0]).wait()
    arrive(OG, ogv.at[0])

    @pl.loop(0, 4)
    def _(i):
        dz = 1 + 2 * i - 3 * (i // 2)
        zh_head = lax.rem(zh + dz, 4)
        two = wv[zh_head].reshape(2 * HDH, D)
        made = lax.dot_general(ogv[...].reshape(2 * T, D), two, NT, preferred_element_type=F32).astype(BF16)
        for e in (0, 1):
            head = zh_head * 4 + 2 * core + e
            for c in (0, 1):
                piece = cgo.at[c, 2 * zh_head + e]
                piece[...] = made[c * T : (c + 1) * T, e * HDH : (e + 1) * HDH]
                stays = jnp.logical_and(core == c, head == f)

                @pl.when(stays)
                def _():
                    pltpu.make_async_copy(piece, cb.at[f], rs.at[CG]).start()

                @pl.when(jnp.logical_not(stays))
                def _():
                    send(piece, cb.at[f], CG, on_core(c, head))

    arrive(CG, cb)

    def backward(t):
        p = probs[t]
        gain = cb[t]
        prob_grad = lax.dot_general(both(vb, t), gain, NT, preferred_element_type=F32)
        score_grad = p * (prob_grad - jnp.sum(prob_grad * p, axis=0, keepdims=True))
        term = jnp.sum((score_grad * plain[t]).reshape(32, 8, HDH), axis=0)
        low = score_grad.astype(BF16)
        query = lax.dot_general(low, both(kb, t), TN, preferred_element_type=F32) * factor
        key = jnp.dot(low, qb[t], preferred_element_type=F32) * factor
        value = jnp.dot(p.astype(BF16), gain, preferred_element_type=F32)
        kp[0, t], kp[1, t] = key[:T], key[T:]
        vp[0, t], vp[1, t] = value[:T], value[T:]
        qo[t] = query.astype(BF16)
        return term

    redo[0] = jnp.zeros((8, HDH), F32)

    @pl.loop(0, F - 1)
    def _(i):
        t = turn(i)
        redo[0] += backward(t)
        send(qo.at[t], qg.at[:, mine], QG, (d, t))

    total = jnp.sum(redo[0] + backward(f), keepdims=True) * inv_root
    pltpu.make_async_copy(qo.at[f], qg.at[:, mine], ls.at[1]).start()

    lanes = lax.broadcasted_iota(jnp.int32, (8, HDH), 1)
    stages = (
        (2, core, [sibling]),
        (4, x, [at_x(i) for i in (1, 2, 3)]),
        (4, y, [at_y(i) for i in (1, 2, 3)]),
        (4, zh, [at_zh(i) for i in (1, 2, 3)]),
        (4, zl, [at_z(i) for i in (1, -1, 2)]),
    )

    def give(s, value):
        _, here, devices = stages[s]
        redo[s + 1] = value
        red[s, here] = value
        for device in devices:
            send(redo.at[s + 1], red.at[s, here], RED + s, device)

    def take(s):
        n, _, devices = stages[s]
        arrive(RED + s, red.at[s, pl.ds(0, len(devices))])
        return sum(red[s, j] for j in range(1, n)) + red[s, 0]

    give(0, jnp.where(lanes == f, total, 0.0))

    def gather(part, out, dst, sem, local):
        def one(g):
            acc = part[0, g]
            for t in range(F):
                acc += jnp.where(pat[1, t] == g, 1.0, 0.0) * part[1, t]
            out[g] = acc.astype(BF16)

        @pl.loop(0, F - 1)
        def _(i):
            g = turn(i)
            one(g)
            send(out.at[g], dst.at[:, mine], sem, (d, g))

        one(f)
        pltpu.make_async_copy(out.at[f], dst.at[:, mine], ls.at[local]).start()

    gather(kp, ko, kg, KG, 2)
    give(1, take(0))
    gather(vp, vo, vg, VG, 3)
    give(2, take(1))

    arrive(CX, cxr)
    width = 512

    @pl.loop(0, D // width)
    def _(n):
        cols = pl.ds(pl.multiple_of(n * width, width), width)
        block = wv[:, :, :, :, cols].reshape(F // 2 * HDH, width)
        made = jnp.dot(cxr[...].reshape(2 * T, F // 2 * HDH), block, preferred_element_type=F32)
        attp[:, :, cols] = made.reshape(2, T, width)

    send(attp.at[1 - core], attr, ATT, sibling)

    arrive(ATT, attr)
    attv[...] = (attp[core] + attr[...]).astype(BF16)
    pltpu.make_async_copy(attv, att, ls.at[4]).start()
    give(3, take(2))
    give(4, take(3))
    sg[...] = take(4)[:1, :F]

    for sem, ref in ((QG, qg), (KG, kg), (VG, vg)):
        arrive(sem, ref.at[:, pl.ds(0, (F - 1) * HDH)])
    for j, (src, dst) in enumerate(((qo, qg), (ko, kg), (vo, vg))):
        pltpu.make_async_copy(src.at[f], dst.at[:, mine], ls.at[j + 1]).wait()
    pltpu.make_async_copy(attv, att, ls.at[4]).wait()
    for sem, ref in ((Q, qb), (K, kb), (V, vb), (QG, qo), (KG, ko), (VG, vo)):
        sent(sem, ref.at[pl.ds(0, F - 1)])

    def sent_but_own(stays, sem, ref, n):
        @pl.when(stays)
        def _():
            sent(sem, ref.at[pl.ds(0, n)])

        @pl.when(jnp.logical_not(stays))
        def _():
            sent(sem, ref)

    sent_but_own(core == y // 2, CG, cb, F - 1)
    sent_but_own(core == y // 2, CX, cxo, F - 1)
    sent_but_own(core == keeper, A, wv.at[0, 0, 0], 48)
    sent(OG, ogv.at[0])
    sent(ATT, attr)
    sent(B1Y, wv.at[0, :, :, pl.ds(0, 48), first])
    sent(B1X, wv.at[pl.ds(0, 3), :, :, pl.ds(0, 16), second])
    for i in range(3):
        sent(B2X + i, wv.at[0, :, :, :, first])
        sent(B2Y + i, wv.at[:, :, :, pl.ds(0, 16), second])
    for s, (_, _, devices) in enumerate(stages):
        sent(RED + s, red.at[s, pl.ds(0, len(devices))])


def local(queries, key_states, value_states, head_scale, out_weight, frame_pattern, out_grad):
    anywhere = pl.BlockSpec(memory_space=pl.ANY)
    scalars = pl.BlockSpec(memory_space=pltpu.SMEM)
    slots = pltpu.VMEM((F, T, HDH), BF16)
    parts = pltpu.VMEM((2, F, T, HDH), F32)
    square = pltpu.VMEM((F, 2 * T, T), F32)
    row = jax.ShapeDtypeStruct((T, F * HDH), BF16)
    attended, query_grad, key_grad, value_grad, scale_grad = pl.pallas_call(
        body,
        out_shape=(
            jax.ShapeDtypeStruct((T, D), BF16),
            row,
            row,
            row,
            jax.ShapeDtypeStruct((1, F), F32),
        ),
        in_specs=[scalars, scalars] + [anywhere] * 5,
        out_specs=[anywhere] * 4 + [pl.BlockSpec(memory_space=pltpu.VMEM)],
        scratch_shapes=[
            pltpu.VMEM((4, 2, 2, 64, D), BF16),
            pltpu.VMEM((2, T, D), BF16),
            slots, slots, slots, slots,
            pltpu.VMEM((2, F // 2, T, HDH), BF16),
            slots,
            pltpu.VMEM((2, T, F // 2 * HDH), BF16),
            slots, slots, slots,
            parts, parts,
            square, square,
            pltpu.VMEM((2, T, D), F32),
            pltpu.VMEM((T, D), F32),
            pltpu.VMEM((T, D), BF16),
            pltpu.VMEM((5, 4, 8, HDH), F32),
            pltpu.VMEM((6, 8, HDH), F32),
            pltpu.SemaphoreType.DMA((N_SEM,)),
            pltpu.SemaphoreType.DMA((N_SEM,)),
            pltpu.SemaphoreType.DMA((5,)),
        ],
        compiler_params=pltpu.CompilerParams(
            collective_id=0, has_side_effects=True, vmem_limit_bytes=56 << 20
        ),
    )(
        frame_pattern.T,
        head_scale,
        queries[0, 0],
        key_states[0, 0],
        value_states[0, 0],
        out_grad[0, 0],
        out_weight,
    )
    return (
        attended[None, None],
        query_grad[None, None],
        key_grad[None, None],
        value_grad[None, None],
        scale_grad.reshape(F),
    )


def solution(mesh):
    rows = P("dp", "frame", None, None)
    return jax.shard_map(
        local,
        mesh=mesh,
        in_specs=(rows, rows, rows, P(), P("dp", None), P(), rows),
        out_specs=(rows, rows, rows, rows, P()),
        check_vma=False,
    )
```

time: 242 us -> 226 us (0.934)
  the two profiles are of different devices: /device:TPU:22 before, /device:TPU:1 now
where the time goes in v2:
time: 226 us; the launch traced here: 225 us
  Pallas kernels  218 us (96%)
  local copies, waits for them, and re-layouts  5.89 us (3%)
    pallas_call x1, Pallas kernels, local(): pl.pallas_call(body, out_shape=(jax.ShapeDtypeStruct((T, D), BF16), row,...  218 us
    unnamed x13, local copies, waits for them, and re-layouts  5.89 us

profile of v2, /device:TPU:1, one launch (start us, length us, event | category | flops | bytes accessed | tf_op | source)
XLA Modules:
  0.0 224.8 jit_solution(18180590997645765619)
XLA Ops:
  0.6 218.3 %shard_map.110 = (bf16[128,3072]{1,0:T(8,128)(2,1)}, bf16[128,2048]{1,0:T(8,128)(2,1)}, bf16[128,2048]{1,0:T(8,128)(2,1)}, bf16[128,2048]{1,0:T(8,128)(2,1)}, f32[1,16]{1,0:T(1,128)}) custom-call(s32[2,16]{1,0:T(2,128)} %bitcast.18, f32[16]{0:T(128)} %scale.1, bf16[128,2048]{1,0:T(8,128)(2,1)} %bitcast.15, bf16[128,2048]{1,0:T(8,128)(2,1)} %bitcast.16, ...), custom_call_target="tpu_custom_call" | custom-call | tf_op jit(solution)/shard_map/pallas_call | solution.py:326
  218.9 0.0 copy-start.2
  218.9 2.1 copy.17
  221.0 0.0 copy-done.2
  221.0 0.0 copy-start.1
  221.0 0.8 copy.18
  221.8 0.4 copy-done.1
  222.3 0.0 copy-start
  222.3 0.8 copy.19
  223.1 0.4 copy-done
  223.5 0.0 copy-start.3
  223.5 0.8 copy.20
  224.3 0.0 copy-done.3
  224.3 0.5 copy.21
Async XLA Ops:
  218.9 2.1 copy-start.2
  221.0 1.2 copy-start.1
  222.3 1.2 copy-start
  223.5 0.8 copy-start.3

commit v3 on v2

--- a/solution.py
+++ b/solution.py
@@ -18,7 +18,7 @@
 
 A, B1Y, B1X, OG, Q, K, V, CG, CX, ATT, QG, KG, VG = range(13)
 B2X, B2Y, RED = 13, 16, 19
-N_SEM = 24
+N_SEM = 22
 NT = (((1,), (1,)), ((), ()))
 TN = (((0,), (0,)), ((), ()))
 
@@ -36,8 +36,8 @@
     def at_frame(i):
         return (d, lax.rem(f + i, F))
 
-    def at_x(i):
-        return (lax.rem(x + i + 4, 4) * 8 + lax.rem(d, 8), f)
+    def at_x(i, other=0):
+        return (lax.rem(x + i + 4, 4) * 8 + zl * 2 + (1 - core if other else core), f)
 
     def at_y(i):
         return (d, zh * 4 + lax.rem(y + i + 4, 4))
@@ -71,7 +71,7 @@
         pltpu.make_async_copy(ref, ref, ss.at[sem]).wait()
 
     barrier = pltpu.get_barrier_semaphore()
-    peers = [at_x(i) for i in (1, 2, 3)] + [at_z(i, c) for i in (1, -1, 2, -2) for c in (0, 1)] + [sibling]
+    peers = [at_x(i, c) for i in (1, 2, 3) for c in (0, 1)] + [at_z(i, c) for i in (1, -1, 2, -2) for c in (0, 1)] + [sibling]
 
     @pl.loop(1, F)
     def _(i):
@@ -112,12 +112,12 @@
         pltpu.make_async_copy(src.at[:, mine], dst.at[f], rs.at[sem]).start()
 
     scatter(q, qb, Q)
+    scatter(k, kb, K)
 
     arrive(A, wv.at[x, :, :, rows])
     for i in (1, 2, 3):
         send(wv.at[x, :, :, rows, first], wv.at[x, :, :, rows, first], B1Y, at_y(i))
         send(wv.at[x, :, :, rows, second], wv.at[x, :, :, rows, second], B1X, at_x(i))
-    scatter(k, kb, K)
 
     arrive(B1Y, wv.at[x, :, :, pl.ds(0, 48), first])
     for i in (1, 2, 3):
@@ -145,27 +145,6 @@
         scaled = scores * factor
         e = jnp.exp(scaled - jnp.max(scaled, axis=0, keepdims=True))
         probs[t] = e / jnp.sum(e, axis=0, keepdims=True)
-
-    arrive(V, vb)
-
-    def forward(t):
-        return lax.dot_general(probs[t].astype(BF16), both(vb, t), TN, preferred_element_type=F32).astype(BF16)
-
-    @pl.loop(0, F - 1)
-    def _(i):
-        t = turn(i)
-        cxo[t] = forward(t)
-        send(cxo.at[t], cxr.at[core, :, here], CX, on_core(y // 2, t))
-
-    cxo[f] = forward(f)
-
-    @pl.when(core == y // 2)
-    def _():
-        pltpu.make_async_copy(cxo.at[f], cxr.at[core, :, here], rs.at[CX]).start()
-
-    @pl.when(core != y // 2)
-    def _():
-        send(cxo.at[f], cxr.at[core, :, here], CX, sibling)
 
     for i in (1, 2, 3):
         arrive(B2X + i - 1, wv.at[0, :, :, :, first])
@@ -193,6 +172,27 @@
                 @pl.when(jnp.logical_not(stays))
                 def _():
                     send(piece, cb.at[f], CG, on_core(c, head))
+
+    arrive(V, vb)
+
+    def forward(t):
+        return lax.dot_general(probs[t].astype(BF16), both(vb, t), TN, preferred_element_type=F32).astype(BF16)
+
+    @pl.loop(0, F - 1)
+    def _(i):
+        t = turn(i)
+        cxo[t] = forward(t)
+        send(cxo.at[t], cxr.at[core, :, here], CX, on_core(y // 2, t))
+
+    cxo[f] = forward(f)
+
+    @pl.when(core == y // 2)
+    def _():
+        pltpu.make_async_copy(cxo.at[f], cxr.at[core, :, here], rs.at[CX]).start()
+
+    @pl.when(core != y // 2)
+    def _():
+        send(cxo.at[f], cxr.at[core, :, here], CX, sibling)
 
     arrive(CG, cb)
 
@@ -224,10 +224,8 @@
 
     lanes = lax.broadcasted_iota(jnp.int32, (8, HDH), 1)
     stages = (
-        (2, core, [sibling]),
-        (4, x, [at_x(i) for i in (1, 2, 3)]),
-        (4, y, [at_y(i) for i in (1, 2, 3)]),
-        (4, zh, [at_zh(i) for i in (1, 2, 3)]),
+        (F, f, [at_frame(i) for i in range(1, F)]),
+        (8, x * 2 + core, [at_x(i, c) for i in range(4) for c in (0, 1) if (i, c) != (0, 0)]),
         (4, zl, [at_z(i) for i in (1, -1, 2)]),
     )
 
@@ -245,6 +243,18 @@
 
     give(0, jnp.where(lanes == f, total, 0.0))
 
+    arrive(CX, cxr)
+    width = 512
+
+    @pl.loop(0, D // width)
+    def _(n):
+        cols = pl.ds(pl.multiple_of(n * width, width), width)
+        block = wv[:, :, :, :, cols].reshape(F // 2 * HDH, width)
+        made = jnp.dot(cxr[...].reshape(2 * T, F // 2 * HDH), block, preferred_element_type=F32)
+        attp[:, :, cols] = made.reshape(2, T, width)
+
+    send(attp.at[1 - core], attr, ATT, sibling)
+
     def gather(part, out, dst, sem, local):
         def one(g):
             acc = part[0, g]
@@ -266,30 +276,16 @@
     gather(vp, vo, vg, VG, 3)
     give(2, take(1))
 
-    arrive(CX, cxr)
-    width = 512
-
-    @pl.loop(0, D // width)
-    def _(n):
-        cols = pl.ds(pl.multiple_of(n * width, width), width)
-        block = wv[:, :, :, :, cols].reshape(F // 2 * HDH, width)
-        made = jnp.dot(cxr[...].reshape(2 * T, F // 2 * HDH), block, preferred_element_type=F32)
-        attp[:, :, cols] = made.reshape(2, T, width)
-
-    send(attp.at[1 - core], attr, ATT, sibling)
-
     arrive(ATT, attr)
     attv[...] = (attp[core] + attr[...]).astype(BF16)
-    pltpu.make_async_copy(attv, att, ls.at[4]).start()
-    give(3, take(2))
-    give(4, take(3))
-    sg[...] = take(4)[:1, :F]
+    pltpu.make_async_copy(attv, att, ls.at[0]).start()
+    sg[...] = take(2)[:1, :F]
 
     for sem, ref in ((QG, qg), (KG, kg), (VG, vg)):
         arrive(sem, ref.at[:, pl.ds(0, (F - 1) * HDH)])
     for j, (src, dst) in enumerate(((qo, qg), (ko, kg), (vo, vg))):
         pltpu.make_async_copy(src.at[f], dst.at[:, mine], ls.at[j + 1]).wait()
-    pltpu.make_async_copy(attv, att, ls.at[4]).wait()
+    pltpu.make_async_copy(attv, att, ls.at[0]).wait()
     for sem, ref in ((Q, qb), (K, kb), (V, vb), (QG, qo), (KG, ko), (VG, vo)):
         sent(sem, ref.at[pl.ds(0, F - 1)])
 
@@ -316,6 +312,21 @@
         sent(RED + s, red.at[s, pl.ds(0, len(devices))])
 
 
+def settle(*refs):
+    scale, scale_out, sems = refs[4], refs[9], refs[14]
+    arrays = list(zip(refs[:4], refs[10:14], refs[5:9]))
+    copies = [pltpu.make_async_copy(src, held, sems.at[0, j]) for j, (src, held, _) in enumerate(arrays)]
+    copies_out = [pltpu.make_async_copy(held, dst, sems.at[1, j]) for j, (_, held, dst) in enumerate(arrays)]
+    for copy in copies:
+        copy.start()
+    scale_out[...] = scale[...]
+    for copy, copy_out in zip(copies, copies_out):
+        copy.wait()
+        copy_out.start()
+    for copy_out in copies_out:
+        copy_out.wait()
+
+
 def local(queries, key_states, value_states, head_scale, out_weight, frame_pattern, out_grad):
     anywhere = pl.BlockSpec(memory_space=pl.ANY)
     scalars = pl.BlockSpec(memory_space=pltpu.SMEM)
@@ -323,17 +334,13 @@
     parts = pltpu.VMEM((2, F, T, HDH), F32)
     square = pltpu.VMEM((F, 2 * T, T), F32)
     row = jax.ShapeDtypeStruct((T, F * HDH), BF16)
-    attended, query_grad, key_grad, value_grad, scale_grad = pl.pallas_call(
+    out_shape = (jax.ShapeDtypeStruct((T, D), BF16), row, row, row, jax.ShapeDtypeStruct((1, F), F32))
+    vector = pl.BlockSpec(memory_space=pltpu.VMEM)
+    made = pl.pallas_call(
         body,
-        out_shape=(
-            jax.ShapeDtypeStruct((T, D), BF16),
-            row,
-            row,
-            row,
-            jax.ShapeDtypeStruct((1, F), F32),
-        ),
+        out_shape=out_shape,
         in_specs=[scalars, scalars] + [anywhere] * 5,
-        out_specs=[anywhere] * 4 + [pl.BlockSpec(memory_space=pltpu.VMEM)],
+        out_specs=[anywhere] * 4 + [vector],
         scratch_shapes=[
             pltpu.VMEM((4, 2, 2, 64, D), BF16),
             pltpu.VMEM((2, T, D), BF16),
@@ -347,11 +354,11 @@
             pltpu.VMEM((2, T, D), F32),
             pltpu.VMEM((T, D), F32),
             pltpu.VMEM((T, D), BF16),
-            pltpu.VMEM((5, 4, 8, HDH), F32),
-            pltpu.VMEM((6, 8, HDH), F32),
+            pltpu.VMEM((3, F, 8, HDH), F32),
+            pltpu.VMEM((4, 8, HDH), F32),
             pltpu.SemaphoreType.DMA((N_SEM,)),
             pltpu.SemaphoreType.DMA((N_SEM,)),
-            pltpu.SemaphoreType.DMA((5,)),
+            pltpu.SemaphoreType.DMA((4,)),
         ],
         compiler_params=pltpu.CompilerParams(
             collective_id=0, has_side_effects=True, vmem_limit_bytes=56 << 20
@@ -365,6 +372,14 @@
         out_grad[0, 0],
         out_weight,
     )
+    attended, query_grad, key_grad, value_grad, scale_grad = pl.pallas_call(
+        settle,
+        out_shape=out_shape,
+        in_specs=[anywhere] * 4 + [vector],
+        out_specs=[anywhere] * 4 + [vector],
+        scratch_shapes=[pltpu.VMEM((T, D), BF16)] + [pltpu.VMEM((T, F * HDH), BF16)] * 3 + [pltpu.SemaphoreType.DMA((2, 4))],
+        compiler_params=pltpu.CompilerParams(vmem_limit_bytes=56 << 20),
+    )(*made)
     return (
         attended[None, None],
         query_grad[None, None],

time: 226 us -> 221 us (0.978)
  local copies, waits for them, and re-layouts: 5.89 us -> 0 us
    unnamed x13 -> x0, local copies, waits for them, and re-layouts: 5.89 us -> none
    pallas_call x1 -> x2, Pallas kernels: 218 us -> 220 us  [the longest x1 216 us: local(): pl.pallas_call(body, out_shape=out_shape, in_specs=[scalars, scalars] + [...]
where the time goes in v3:
time: 221 us; the launch traced here: 220 us
  Pallas kernels  220 us (100%)
    pallas_call x1, Pallas kernels, local(): pl.pallas_call(body, out_shape=out_shape, in_specs=[scalars, scalars] + [...  216 us

profile of v3, /device:TPU:1, one launch (start us, length us, event | category | flops | bytes accessed | tf_op | source)
XLA Modules:
  0.0 220.3 jit_solution(15538992026074466256)
XLA Ops:
  0.6 215.9 %shard_map.110 = (bf16[128,3072]{1,0:T(8,128)(2,1)}, bf16[128,2048]{1,0:T(8,128)(2,1)}, bf16[128,2048]{1,0:T(8,128)(2,1)}, bf16[128,2048]{1,0:T(8,128)(2,1)}, f32[1,16]{1,0:T(1,128)}) custom-call(s32[2,16]{1,0:T(2,128)} %bitcast.14, f32[16]{0:T(128)} %scale.1, bf16[128,2048]{1,0:T(8,128)(2,1)} %bitcast.11, bf16[128,2048]{1,0:T(8,128)(2,1)} %bitcast.12, ...), custom_call_target="tpu_custom_call" | custom-call | tf_op jit(solution)/shard_map/pallas_call | solution.py:339
  216.6 3.8 %shard_map.111 = (bf16[128,3072]{1,0:T(8,128)(2,1)}, bf16[128,2048]{1,0:T(8,128)(2,1)}, bf16[128,2048]{1,0:T(8,128)(2,1)}, bf16[128,2048]{1,0:T(8,128)(2,1)}, f32[1,16]{1,0:T(1,128)}) custom-call(bf16[128,3072]{1,0:T(8,128)(2,1)} %get-tuple-element.15.refs_0_, bf16[128,2048]{1,0:T(8,128)(2,1)} %get-tuple-element.16.refs_1_, ...), custom_call_target="tpu_custom_call" | custom-call | tf_op jit(solution)/shard_map/pallas_call | solution.py:375

commit v4 on v3

--- a/solution.py
+++ b/solution.py
@@ -314,7 +314,8 @@
 
 def settle(*refs):
     scale, scale_out, sems = refs[4], refs[9], refs[14]
-    arrays = list(zip(refs[:4], refs[10:14], refs[5:9]))
+    halves = [pl.ds(n * T // 2, T // 2) for n in (0, 1)]
+    arrays = [(i.at[n], v.at[n], o.at[n]) for i, v, o in zip(refs[:4], refs[10:14], refs[5:9]) for n in halves]
     copies = [pltpu.make_async_copy(src, held, sems.at[0, j]) for j, (src, held, _) in enumerate(arrays)]
     copies_out = [pltpu.make_async_copy(held, dst, sems.at[1, j]) for j, (_, held, dst) in enumerate(arrays)]
     for copy in copies:
@@ -377,7 +378,7 @@
         out_shape=out_shape,
         in_specs=[anywhere] * 4 + [vector],
         out_specs=[anywhere] * 4 + [vector],
-        scratch_shapes=[pltpu.VMEM((T, D), BF16)] + [pltpu.VMEM((T, F * HDH), BF16)] * 3 + [pltpu.SemaphoreType.DMA((2, 4))],
+        scratch_shapes=[pltpu.VMEM((T, D), BF16)] + [pltpu.VMEM((T, F * HDH), BF16)] * 3 + [pltpu.SemaphoreType.DMA((2, 8))],
         compiler_params=pltpu.CompilerParams(vmem_limit_bytes=56 << 20),
     )(*made)
     return (

time: 221 us -> 221 us (level)
  no operation moved by 1% of the time
where the time goes in v4:
time: 221 us; the launch traced here: 220 us
  Pallas kernels  220 us (100%)
    pallas_call x1, Pallas kernels, local(): pl.pallas_call(body, out_shape=out_shape, in_specs=[scalars, scalars] + [...  216 us

profile of v4, /device:TPU:1, one launch (start us, length us, event | category | flops | bytes accessed | tf_op | source)
XLA Modules:
  0.0 220.3 jit_solution(16612123814612964515)
XLA Ops:
  0.6 215.9 %shard_map.110 = (bf16[128,3072]{1,0:T(8,128)(2,1)}, bf16[128,2048]{1,0:T(8,128)(2,1)}, bf16[128,2048]{1,0:T(8,128)(2,1)}, bf16[128,2048]{1,0:T(8,128)(2,1)}, f32[1,16]{1,0:T(1,128)}) custom-call(s32[2,16]{1,0:T(2,128)} %bitcast.14, f32[16]{0:T(128)} %scale.1, bf16[128,2048]{1,0:T(8,128)(2,1)} %bitcast.11, bf16[128,2048]{1,0:T(8,128)(2,1)} %bitcast.12, ...), custom_call_target="tpu_custom_call" | custom-call | tf_op jit(solution)/shard_map/pallas_call | solution.py:340
  216.6 3.7 %shard_map.111 = (bf16[128,3072]{1,0:T(8,128)(2,1)}, bf16[128,2048]{1,0:T(8,128)(2,1)}, bf16[128,2048]{1,0:T(8,128)(2,1)}, bf16[128,2048]{1,0:T(8,128)(2,1)}, f32[1,16]{1,0:T(1,128)}) custom-call(bf16[128,3072]{1,0:T(8,128)(2,1)} %get-tuple-element.15.refs_0_, bf16[128,2048]{1,0:T(8,128)(2,1)} %get-tuple-element.16.refs_1_, ...), custom_call_target="tpu_custom_call" | custom-call | tf_op jit(solution)/shard_map/pallas_call | solution.py:376
